TPU v7x, 128 devices: a whole 4x4x4 slice. The times are simulated.
128 devices in a mesh: pop: 8 (over x, core), unit: 16 (over z, y).
Axes of the slice: x: 4, y: 4, z: 4, core: 2. Of those that a mesh axis runs over, the one named last changes fastest.
Arguments:
- states: bfloat16 [4, 4096, 1024], P(None, 'unit', 'pop'), may hold values from -6 to 6
- gate_inputs: bfloat16 [4, 3, 4096, 1024], P(None, None, 'unit', 'pop'), may hold values from -6 to 6
- actions: bfloat16 [4, 128, 1024], P(None, None, 'pop'), may hold values from -0.8984375 to 0.8984375
- final_grad: bfloat16 [4096, 1024], P('unit', 'pop'), may hold values from -6 to 6
- recur_weight: bfloat16 [4096, 3, 4096], P(None, None, 'unit'), may hold values from -0.09375 to 0.09375
- act_weight: bfloat16 [128, 3, 4096], P(None, None, 'unit'), may hold values from -0.5 to 0.5
- opp_first: bfloat16 [32, 4096, 4096], P('pop', None, 'unit'), may hold values from -0.09375 to 0.09375
- opp_second: bfloat16 [32, 128, 4096], P('pop'), may hold values from -0.09375 to 0.09375
- opponent: int32 [1024, 1], P('pop'), may hold values from 0 to 31; in each aligned block of 128 rows (0 to 127, 128 to 255, ...) at most 12 rows name the same one
Outputs:
- start_grad: bfloat16 [4096, 1024], P('unit', 'pop')
- act_weight_grad: float32 [128, 3, 4096], P(None, None, 'unit')
Inputs may be any that keep to these rules, and one draw needn't show every extreme that they name: In each aligned block of 128 rows (the rows of one index of pop) no opponent is named by more than 12 rows, a bound that some block reaches.
All inputs are finite; a program needn't handle non-finite values.
Results may differ from a plain program's by a relative error of at most 0.02.
Values may be sent and summed in bfloat16 or wider, within the bound.
A program may use at most 128 MiB of HBM per device.

v0:
```python
import jax
import jax.numpy as jnp
from jax import lax
from jax.sharding import PartitionSpec as P

CAP = 12


def gru_backward(gradient, pre_gates, latent):
    reset = jax.nn.sigmoid(pre_gates[0].astype(jnp.float32))
    cand_input = pre_gates[1].astype(jnp.float32)
    update = jax.nn.sigmoid(pre_gates[2].astype(jnp.float32) - 1.0)
    candidate = jnp.tanh(reset * cand_input)
    grad_cand = gradient * update * (1.0 - candidate * candidate)
    grad_reset = grad_cand * cand_input * reset * (1.0 - reset)
    grad_input = grad_cand * reset
    grad_update = gradient * (candidate - latent.astype(jnp.float32)) * update * (1.0 - update)
    direct = gradient * (1.0 - update)
    return (direct, jnp.stack([grad_reset, grad_input, grad_update]).astype(jnp.bfloat16))


def silu_slope(values):
    logistic = jax.nn.sigmoid(values)
    return logistic * (1.0 + values * (1.0 - logistic))


def hidden_slope(received, opp_first):
    members_here = received.shape[1]
    partial_sum = jnp.concatenate(
        [
            jnp.dot(opp_first[member], received[:, member, :], preferred_element_type=jnp.float32)
            for member in range(members_here)
        ],
        axis=1,
    )
    summed = lax.psum(partial_sum.astype(jnp.bfloat16), "unit").astype(jnp.float32)
    return silu_slope(summed)


def opponent_backward(slope, incoming, opp_first, opp_second):
    members_here = incoming.shape[1]
    slot_count = incoming.shape[2]
    upward = jnp.concatenate(
        [
            jnp.dot(
                opp_second[member].T, incoming[:, member, :], preferred_element_type=jnp.float32
            )
            for member in range(members_here)
        ],
        axis=1,
    )
    scaled = (upward * slope).astype(jnp.bfloat16)
    backward = jnp.concatenate(
        [
            jnp.dot(
                opp_first[member].T,
                scaled[:, member * slot_count : (member + 1) * slot_count],
                preferred_element_type=jnp.float32,
            )
            for member in range(members_here)
        ],
        axis=1,
    )
    return backward.astype(jnp.bfloat16).reshape(opp_first.shape[2], members_here, slot_count)


def body(
    states,
    gate_inputs,
    actions,
    final_grad,
    recur_weight,
    act_weight,
    opp_first,
    opp_second,
    opponent,
):
    step_count = states.shape[0]
    share = states.shape[1]
    row_count = states.shape[2]
    groups = lax.axis_size("pop")
    members_here = opp_first.shape[0]
    slot_count = groups * CAP
    population = members_here * groups
    chosen = opponent[:, 0]
    onehot = (chosen[:, None] == jnp.arange(population, dtype=jnp.int32)[None, :]).astype(jnp.int32)
    position = jnp.sum((jnp.cumsum(onehot, axis=0) - onehot) * onehot, axis=1)
    column = chosen % members_here * slot_count + chosen // members_here * CAP + position
    packing = (
        column[:, None] == jnp.arange(members_here * slot_count, dtype=jnp.int32)[None, :]
    ).astype(jnp.bfloat16)

    def pack_rows(values):
        packed = jnp.dot(values, packing, preferred_element_type=jnp.float32).astype(jnp.bfloat16)
        return packed.reshape(values.shape[0], members_here, slot_count)

    recur_flat = recur_weight.reshape(recur_weight.shape[0], -1)
    action_flat = act_weight.reshape(act_weight.shape[0], -1)
    gradient = final_grad.astype(jnp.float32)
    weight_grad = jnp.zeros(action_flat.shape, jnp.float32)
    for step in reversed(range(step_count)):
        direct, pre_grads = gru_backward(gradient, gate_inputs[step], states[step])
        flat_grads = pre_grads.reshape(-1, row_count)
        carried = lax.psum_scatter(
            jnp.dot(recur_flat, flat_grads, preferred_element_type=jnp.float32).astype(
                jnp.bfloat16
            ),
            "unit",
            scatter_dimension=0,
            tiled=True,
        ).astype(jnp.float32)
        action_grad = lax.psum(
            jnp.dot(action_flat, flat_grads, preferred_element_type=jnp.float32).astype(
                jnp.bfloat16
            ),
            "unit",
        ).astype(jnp.float32)
        weight_grad = weight_grad + jnp.dot(
            actions[step], flat_grads.T, preferred_element_type=jnp.float32
        )
        taken = actions[step].astype(jnp.float32)
        policy_grad = (action_grad * (1.0 - taken * taken)).astype(jnp.bfloat16)
        packed_grad = pack_rows(policy_grad)
        arrived_state, incoming = (
            lax.all_to_all(pack_rows(states[step]), "pop", split_axis=2, concat_axis=2, tiled=True),
            lax.all_to_all(packed_grad, "pop", split_axis=2, concat_axis=2, tiled=True),
        )
        slope = hidden_slope(arrived_state, opp_first)
        returned = lax.all_to_all(
            opponent_backward(slope, incoming, opp_first, opp_second),
            "pop",
            split_axis=2,
            concat_axis=2,
            tiled=True,
        )
        from_opponent = jnp.dot(
            returned.reshape(share, -1), packing.T, preferred_element_type=jnp.float32
        )
        gradient = direct + carried + from_opponent
    summed_weight = lax.psum(weight_grad.astype(jnp.bfloat16), "pop").astype(jnp.float32)
    return (gradient.astype(jnp.bfloat16), summed_weight.reshape(act_weight.shape))


def solution(mesh):
    placed = (
        P(None, "unit", "pop"),
        P(None, None, "unit", "pop"),
        P(None, None, "pop"),
        P("unit", "pop"),
        P(None, None, "unit"),
        P(None, None, "unit"),
        P("pop", None, "unit"),
        P("pop", None, None),
        P("pop", None),
    )
    return jax.shard_map(
        body,
        mesh=mesh,
        in_specs=placed,
        out_specs=(P("unit", "pop"), P(None, None, "unit")),
        check_vma=False,
    )
```

profile of v0, /device:TPU:0, one launch (start us, length us, event | category | flops | bytes accessed | tf_op | source)
XLA Modules:
  0.0 733.9 jit_solution(13641392170880029019)
XLA Ops:
  11.7 4.4 all-to-all-start.1
  22.9 4.0 all-to-all-start.4
  34.2 2.4 fusion.39
  37.3 4.8 all-to-all-start.7
  43.7 3.2 fusion.40
  47.0 3.3 fusion.41
  50.2 3.3 fusion.42
  53.5 3.3 fusion.43
  56.7 4.8 all-to-all-start.10
  62.2 3.2 fusion.44
  65.4 3.2 fusion.45
  68.7 3.3 fusion.46
  71.9 3.3 fusion.47
  76.8 2.4 fusion.48
  79.2 2.5 fusion.49
  81.7 2.4 fusion.50
  84.1 2.4 fusion.51
  86.5 3.1 pad_maximum_fusion
  90.0 3.0 pad_maximum_fusion.2
  95.4 78.4 %psum.63 = bf16[128,128]{0,1:T(8,128)(2,1)S(1)} all-reduce(bf16[128,128]{0,1:T(8,128)(2,1)S(1)} %fusion.205), channel_id=1, replica_groups=mesh['pop'=8,'unit'=16] {'unit'}, use_global_device_ids=true, to_apply=%region_1.2 | all-reduce | flops 16384 | bytes 65536 | tf_op jit(solution)/shard_map/psum | solution.py:112
  174.9 4.9 all-to-all-start
  180.4 6.1 fusion.35
  204.2 72.7 %all-reduce.6.cloned.1.call-done = (bf16[4096,384]{0,1:T(8,128)(2,1)}, bf16[4096,384]{0,1:T(8,128)(2,1)}, bf16[4096,384]{0,1:T(8,128)(2,1)}, bf16[4096,384]{0,1:T(8,128)(2,1)}) async-done(((bf16[4096,384]{0,1:T(8,128)(2,1)}, bf16[4096,384]{0,1:T(8,128)(2,1)}, bf16[4096,384]{0,1:T(8,128)(2,1)}, bf16[4096,384]{0,1:T(8,128)(2,1)}), (bf16[4096,384]{0,1:T(8,128)(2,1)}, bf16[4096,384]{0,1:T(8,128)(2,1)}, ...) | async-done | bytes 12582928 | tf_op jit(solution)/shard_map/psum | solution.py:36
  276.9 4.4 fusion.6
  290.7 4.3 all-to-all-start.2
  295.2 6.6 all-to-all-done.2
  301.8 51.3 %reduce-scatter.5.cloned.1.call-done = bf16[256,128]{0,1:T(8,128)(2,1)} async-done(((bf16[4096,128]{0,1:T(8,128)(2,1)}), bf16[256,128]{0,1:T(8,128)(2,1)}) %reduce-scatter.5.cloned.1.call-update) | async-done | bytes 65552 | tf_op jit(solution)/shard_map/reduce_scatter | solution.py:104
  354.4 5.9 fusion.34
  360.6 72.2 %psum.65 = bf16[128,128]{0,1:T(8,128)(2,1)S(1)} all-reduce(bf16[128,128]{0,1:T(8,128)(2,1)S(1)} %fusion.204), channel_id=1, replica_groups=mesh['pop'=8,'unit'=16] {'unit'}, use_global_device_ids=true, to_apply=%region_6.7 | all-reduce | flops 16384 | bytes 65536 | tf_op jit(solution)/shard_map/psum | solution.py:112
  433.9 4.5 all-to-all-start.3
  438.6 5.6 all-to-all-done.3
  448.5 2.7 fusion.13
  454.4 3.4 all-to-all-start.5
  458.1 6.5 all-to-all-done.5
  465.9 5.9 fusion.33
  472.1 69.6 %psum.67 = bf16[128,128]{0,1:T(8,128)(2,1)S(1)} all-reduce(bf16[128,128]{0,1:T(8,128)(2,1)S(1)} %fusion.203), channel_id=1, replica_groups=mesh['pop'=8,'unit'=16] {'unit'}, use_global_device_ids=true, to_apply=%region_9.10 | all-reduce | flops 16384 | bytes 65536 | tf_op jit(solution)/shard_map/psum | solution.py:112
  542.8 3.4 all-to-all-start.6
  546.3 5.5 all-to-all-done.6
  556.3 2.7 fusion.20
  562.2 3.4 all-to-all-start.8
  566.0 6.3 all-to-all-done.8
  575.1 69.6 %psum.69 = bf16[128,128]{0,1:T(8,128)(2,1)S(1)} all-reduce(bf16[128,128]{0,1:T(8,128)(2,1)S(1)} %fusion.202), channel_id=1, replica_groups=mesh['pop'=8,'unit'=16] {'unit'}, use_global_device_ids=true, to_apply=%region_12.13 | all-reduce | flops 16384 | bytes 65536 | tf_op jit(solution)/shard_map/psum | solution.py:112
  645.8 3.4 all-to-all-start.9
  649.2 5.9 fusion.32
  659.5 2.7 fusion.27
  665.1 4.7 all-to-all-start.11
  671.5 5.1 all-to-all-done.11
  676.7 48.4 %reduce-scatter.11.cloned.1.call-done = bf16[256,128]{0,1:T(8,128)(2,1)} async-done(((bf16[4096,128]{0,1:T(8,128)(2,1)}), bf16[256,128]{0,1:T(8,128)(2,1)}) %reduce-scatter.11.cloned.1.call-update) | async-done | bytes 65552 | tf_op jit(solution)/shard_map/reduce_scatter | solution.py:104
  (248 shorter events, 90.6 us)
Async XLA Ops:
  7.2 88.0 %copy-start = (bf16[128,3,256]{2,0,1:T(8,128)(2,1)S(1)}, bf16[128,3,256]{2,0,1:T(8,128)(2,1)}, u32[]{:S(2)}) copy-start(bf16[128,3,256]{2,0,1:T(8,128)(2,1)} %param.14) | copy-start | bytes 589828
  11.7 11.2 %all-to-all-start.1 = ((bf16[256,4,96]{0,1,2:T(4,128)(2,1)}), bf16[256,4,96]{0,1,2:T(4,128)(2,1)S(1)}, u32[]{:S(2)}, u32[]{:S(2)}) async-start(bf16[256,4,96]{0,1,2:T(4,128)(2,1)} %copy.140), calls=%async_computation.2 | async-start | bytes 393216 | tf_op jit(solution)/shard_map/all_to_all | solution.py:125
  22.9 13.7 %all-to-all-start.4 = ((bf16[256,4,96]{0,1,2:T(4,128)(2,1)}), bf16[256,4,96]{0,1,2:T(4,128)(2,1)S(1)}, u32[]{:S(2)}, u32[]{:S(2)}) async-start(bf16[256,4,96]{0,1,2:T(4,128)(2,1)} %copy.159), calls=%async_computation.6 | async-start | bytes 393216 | tf_op jit(solution)/shard_map/all_to_all | solution.py:125
  37.3 19.5 %all-to-all-start.7 = ((bf16[256,4,96]{0,1,2:T(4,128)(2,1)}), bf16[256,4,96]{0,1,2:T(4,128)(2,1)S(1)}, u32[]{:S(2)}, u32[]{:S(2)}) async-start(bf16[256,4,96]{0,1,2:T(4,128)(2,1)} %copy.178), calls=%async_computation.10 | async-start | bytes 393216 | tf_op jit(solution)/shard_map/all_to_all | solution.py:125
  56.7 18.5 %all-to-all-start.10 = ((bf16[256,4,96]{0,1,2:T(4,128)(2,1)}), bf16[256,4,96]{0,1,2:T(4,128)(2,1)}, u32[]{:S(2)}, u32[]{:S(2)}) async-start(bf16[256,4,96]{0,1,2:T(4,128)(2,1)} %copy.197), calls=%async_computation.14 | async-start | bytes 393216 | tf_op jit(solution)/shard_map/all_to_all | solution.py:125
  61.6 215.3 %all-reduce.6.cloned.1.call-start = ((), (), s32[]{:S(2)}) async-start(), calls=%async_computation.21 | async-start | bytes 25165824 | tf_op jit(solution)/shard_map/psum | solution.py:36
  79.2 7.3 copy-start.5
  79.2 7.3 copy-start.6
  79.2 7.3 copy-start.7
  79.2 7.3 copy-start.8
  86.5 3.4 copy-start.12
  94.3 92.2 %copy-start.33 = (bf16[1,1,256,128]{2,3,1,0:T(8,128)(2,1)}, bf16[1,1,256,128]{2,3,1,0:T(8,128)(2,1)S(1)}, u32[]{:S(2)}) copy-start(bf16[1,1,256,128]{2,3,1,0:T(8,128)(2,1)S(1)} %copy.215) | copy-start | bytes 196612
  174.9 22.7 %all-to-all-start = ((bf16[128,4,96]{0,1,2:T(4,128)(2,1)}), bf16[128,4,96]{0,1,2:T(4,128)(2,1)S(1)}, u32[]{:S(2)}, u32[]{:S(2)}) async-start(bf16[128,4,96]{0,1,2:T(4,128)(2,1)} %copy.135), calls=%async_computation.1 | async-start | bytes 196608 | tf_op jit(solution)/shard_map/all_to_all | solution.py:126
  179.8 173.4 %reduce-scatter.5.cloned.1.call-start = ((), (), s32[]{:S(2)}) async-start(), calls=%async_computation.16 | async-start | bytes 1114112 | tf_op jit(solution)/shard_map/reduce_scatter | solution.py:104
  197.7 3.5 copy-start.1
  285.5 9.5 %copy-start.20 = (bf16[4,128,128]{2,1,0:T(8,128)(2,1)S(1)}, bf16[4,128,128]{2,1,0:T(8,128)(2,1)}, u32[]{:S(2)}) copy-start(bf16[4,128,128]{2,1,0:T(8,128)(2,1)} %param.11) | copy-start | bytes 393220
  285.5 67.7 %copy-start.34 = (bf16[1,1,256,128]{2,3,1,0:T(8,128)(2,1)S(1)}, bf16[1,1,256,128]{2,3,1,0:T(8,128)(2,1)}, u32[]{:S(2)}) copy-start(bf16[1,1,256,128]{2,3,1,0:T(8,128)(2,1)} %copy-done.33) | copy-start | bytes 196612
  285.5 67.6 %copy-start.36 = (bf16[256,128]{0,1:T(8,128)(2,1)S(1)}, bf16[256,128]{0,1:T(8,128)(2,1)}, u32[]{:S(2)}) copy-start(bf16[256,128]{0,1:T(8,128)(2,1)} %copy-done.35) | copy-start | bytes 196612
  287.7 66.6 %copy-start.26 = (bf16[1,1,256,128]{2,3,1,0:T(8,128)(2,1)S(1)}, bf16[1,1,256,128]{2,3,1,0:T(8,128)(2,1)}, u32[]{:S(2)}) copy-start(bf16[1,1,256,128]{2,3,1,0:T(8,128)(2,1)} %copy.228) | copy-start | bytes 196612
  287.7 66.6 %copy-start.30 = (bf16[1,1,256,128]{2,3,1,0:T(8,128)(2,1)S(1)}, bf16[1,1,256,128]{2,3,1,0:T(8,128)(2,1)}, u32[]{:S(2)}) copy-start(bf16[1,1,256,128]{2,3,1,0:T(8,128)(2,1)} %copy.229) | copy-start | bytes 196612
  287.7 66.6 %copy-start.31 = (bf16[1,1,256,128]{2,3,1,0:T(8,128)(2,1)S(1)}, bf16[1,1,256,128]{2,3,1,0:T(8,128)(2,1)}, u32[]{:S(2)}) copy-start(bf16[1,1,256,128]{2,3,1,0:T(8,128)(2,1)} %copy.230) | copy-start | bytes 196612
  287.7 66.6 %copy-start.32 = (bf16[1,256,128]{1,2,0:T(8,128)(2,1)S(1)}, bf16[1,256,128]{1,2,0:T(8,128)(2,1)}, u32[]{:S(2)}) copy-start(bf16[1,256,128]{1,2,0:T(8,128)(2,1)} %copy.231) | copy-start | bytes 196612
  290.7 11.1 %all-to-all-start.2 = ((bf16[256,4,96]{0,1,2:T(4,128)(2,1)}), bf16[256,4,96]{0,1,2:T(4,128)(2,1)S(1)}, u32[]{:S(2)}, u32[]{:S(2)}) async-start(bf16[256,4,96]{0,1,2:T(4,128)(2,1)} %copy.145), calls=%async_computation.3 | async-start | bytes 393216 | tf_op jit(solution)/shard_map/all_to_all | solution.py:129
  295.0 169.7 %reduce-scatter.7.cloned.1.call-start = ((), (), s32[]{:S(2)}) async-start(), calls=%async_computation.17 | async-start | bytes 1114112 | tf_op jit(solution)/shard_map/reduce_scatter | solution.py:104
  354.4 78.4 %copy-start.39 = (bf16[1,128,128]{1,2,0:T(8,128)(2,1)S(1)}, bf16[1,128,128]{1,2,0:T(8,128)(2,1)}, u32[]{:S(2)}) copy-start(bf16[1,128,128]{1,2,0:T(8,128)(2,1)} %copy.232) | copy-start | bytes 98308
  433.9 10.2 %all-to-all-start.3 = ((bf16[128,4,96]{0,1,2:T(4,128)(2,1)}), bf16[128,4,96]{0,1,2:T(4,128)(2,1)S(1)}, u32[]{:S(2)}, u32[]{:S(2)}) async-start(bf16[128,4,96]{0,1,2:T(4,128)(2,1)} %copy.154), calls=%async_computation.5 | async-start | bytes 196608 | tf_op jit(solution)/shard_map/all_to_all | solution.py:126
  444.1 3.6 copy-start.2
  453.0 12.7 %copy-start.22 = (bf16[1,1,256,128]{2,3,1,0:T(8,128)(2,1)S(1)}, bf16[1,1,256,128]{2,3,1,0:T(8,128)(2,1)}, u32[]{:S(2)}) copy-start(bf16[1,1,256,128]{2,3,1,0:T(8,128)(2,1)} %copy.241) | copy-start | bytes 196612
  453.0 12.7 %copy-start.27 = (bf16[1,1,256,128]{2,3,1,0:T(8,128)(2,1)S(1)}, bf16[1,1,256,128]{2,3,1,0:T(8,128)(2,1)}, u32[]{:S(2)}) copy-start(bf16[1,1,256,128]{2,3,1,0:T(8,128)(2,1)} %copy.242) | copy-start | bytes 196612
  453.1 12.7 %copy-start.28 = (bf16[1,1,256,128]{2,3,1,0:T(8,128)(2,1)S(1)}, bf16[1,1,256,128]{2,3,1,0:T(8,128)(2,1)}, u32[]{:S(2)}) copy-start(bf16[1,1,256,128]{2,3,1,0:T(8,128)(2,1)} %copy.243) | copy-start | bytes 196612
  453.1 12.7 %copy-start.29 = (bf16[1,256,128]{1,2,0:T(8,128)(2,1)S(1)}, bf16[1,256,128]{1,2,0:T(8,128)(2,1)}, u32[]{:S(2)}) copy-start(bf16[1,256,128]{1,2,0:T(8,128)(2,1)} %copy.244) | copy-start | bytes 196612
  454.4 10.2 %all-to-all-start.5 = ((bf16[256,4,96]{0,1,2:T(4,128)(2,1)}), bf16[256,4,96]{0,1,2:T(4,128)(2,1)S(1)}, u32[]{:S(2)}, u32[]{:S(2)}) async-start(bf16[256,4,96]{0,1,2:T(4,128)(2,1)} %copy.164), calls=%async_computation.7 | async-start | bytes 393216 | tf_op jit(solution)/shard_map/all_to_all | solution.py:129
  457.8 114.5 %reduce-scatter.9.cloned.1.call-start = ((), (), s32[]{:S(2)}) async-start(), calls=%async_computation.18 | async-start | bytes 1114112 | tf_op jit(solution)/shard_map/reduce_scatter | solution.py:104
  465.9 75.8 %copy-start.38 = (bf16[1,128,128]{1,2,0:T(8,128)(2,1)S(1)}, bf16[1,128,128]{1,2,0:T(8,128)(2,1)}, u32[]{:S(2)}) copy-start(bf16[1,128,128]{1,2,0:T(8,128)(2,1)} %copy.245) | copy-start | bytes 98308
  542.8 9.1 %all-to-all-start.6 = ((bf16[128,4,96]{0,1,2:T(4,128)(2,1)}), bf16[128,4,96]{0,1,2:T(4,128)(2,1)S(1)}, u32[]{:S(2)}, u32[]{:S(2)}) async-start(bf16[128,4,96]{0,1,2:T(4,128)(2,1)} %copy.173), calls=%async_computation.9 | async-start | bytes 196608 | tf_op jit(solution)/shard_map/all_to_all | solution.py:126
  551.9 3.6 copy-start.3
  560.8 12.7 %copy-start.21 = (bf16[1,1,256,128]{2,3,1,0:T(8,128)(2,1)S(1)}, bf16[1,1,256,128]{2,3,1,0:T(8,128)(2,1)}, u32[]{:S(2)}) copy-start(bf16[1,1,256,128]{2,3,1,0:T(8,128)(2,1)} %copy.254) | copy-start | bytes 196612
  560.8 12.7 %copy-start.23 = (bf16[1,1,256,128]{2,3,1,0:T(8,128)(2,1)S(1)}, bf16[1,1,256,128]{2,3,1,0:T(8,128)(2,1)}, u32[]{:S(2)}) copy-start(bf16[1,1,256,128]{2,3,1,0:T(8,128)(2,1)} %copy.255) | copy-start | bytes 196612
  560.8 12.7 %copy-start.24 = (bf16[1,1,256,128]{2,3,1,0:T(8,128)(2,1)S(1)}, bf16[1,1,256,128]{2,3,1,0:T(8,128)(2,1)}, u32[]{:S(2)}) copy-start(bf16[1,1,256,128]{2,3,1,0:T(8,128)(2,1)} %copy.256) | copy-start | bytes 196612
  560.8 12.7 %copy-start.25 = (bf16[1,256,128]{1,2,0:T(8,128)(2,1)S(1)}, bf16[1,256,128]{1,2,0:T(8,128)(2,1)}, u32[]{:S(2)}) copy-start(bf16[1,256,128]{1,2,0:T(8,128)(2,1)} %copy.257) | copy-start | bytes 196612
  561.3 83.4 %copy-start.37 = (bf16[1,128,128]{1,2,0:T(8,128)(2,1)S(1)}, bf16[1,128,128]{1,2,0:T(8,128)(2,1)}, u32[]{:S(2)}) copy-start(bf16[1,128,128]{1,2,0:T(8,128)(2,1)} %copy.258) | copy-start | bytes 98308
  562.2 10.2 %all-to-all-start.8 = ((bf16[256,4,96]{0,1,2:T(4,128)(2,1)}), bf16[256,4,96]{0,1,2:T(4,128)(2,1)S(1)}, u32[]{:S(2)}, u32[]{:S(2)}) async-start(bf16[256,4,96]{0,1,2:T(4,128)(2,1)} %copy.183), calls=%async_computation.11 | async-start | bytes 393216 | tf_op jit(solution)/shard_map/all_to_all | solution.py:129
  565.6 104.3 %all-reduce.4.cloned.1.call-start = ((), (), s32[]{:S(2)}) async-start(), calls=%async_computation.20 | async-start | bytes 393216 | tf_op jit(solution)/shard_map/psum | solution.py:140
  645.8 9.3 %all-to-all-start.9 = ((bf16[128,4,96]{0,1,2:T(4,128)(2,1)}), bf16[128,4,96]{0,1,2:T(4,128)(2,1)S(1)}, u32[]{:S(2)}, u32[]{:S(2)}) async-start(bf16[128,4,96]{0,1,2:T(4,128)(2,1)} %copy.192), calls=%async_computation.13 | async-start | bytes 196608 | tf_op jit(solution)/shard_map/all_to_all | solution.py:126
  649.1 75.9 %reduce-scatter.11.cloned.1.call-start = ((), (), s32[]{:S(2)}) async-start(), calls=%async_computation.19 | async-start | bytes 1114112 | tf_op jit(solution)/shard_map/reduce_scatter | solution.py:104
  655.1 3.7 copy-start.4
  658.8 3.5 slice-start.4
  665.1 11.5 %all-to-all-start.11 = ((bf16[256,4,96]{0,1,2:T(4,128)(2,1)}), bf16[256,4,96]{0,1,2:T(4,128)(2,1)S(1)}, u32[]{:S(2)}, u32[]{:S(2)}) async-start(bf16[256,4,96]{0,1,2:T(4,128)(2,1)} %copy.202), calls=%async_computation.15 | async-start | bytes 393216 | tf_op jit(solution)/shard_map/all_to_all | solution.py:129
  (17 other events, 39.6 us)
Sparse Core Ops, SparseCore 0:
  93.1 183.7 all-reduce.5
  280.4 72.6 reduce-scatter.4
  360.7 72.2 reduce-scatter.6
  472.2 67.5 reduce-scatter.8
  575.3 53.9 all-reduce.3
  655.2 69.7 reduce-scatter.10
where the time goes:
time: 742 us; the launch traced here: 734 us
  blocking collectives  290 us (39%)
  waiting for transfers between devices  209 us (28%)
  matrix products  114 us (15%)
  starting transfers between devices  51 us (7%)
  local copies, waits for them, and re-layouts  31.5 us (4%)
  other arithmetic  23.6 us (3%)
  between operations  15.5 us (2%)
    psum x4, blocking collectives, body(): lax.psum(jnp.dot(action_flat, flat_grads, preferred_element_type=jnp.floa...  290 us
    reduce_scatter x4, waiting for transfers between devices, body(): lax.psum_scatter(jnp.dot(recur_flat, flat_grads, preferred_element_type=j...  99.7 us
    psum x1, waiting for transfers between devices, hidden_slope(): lax.psum(partial_sum.astype(jnp.bfloat16), 'unit').astype(jnp.float32)  72.7 us
    dot_general x16, matrix products, hidden_slope(): jnp.dot(opp_first[member], received[:, member, :], preferred_element_type...  45 us
    all_to_all x4, waiting for transfers between devices, body(): lax.all_to_all(opponent_backward(slope, incoming, opp_first, opp_second),...  24.5 us
    dot_general x4, matrix products, body(): jnp.dot(recur_flat, flat_grads, preferred_element_type=jnp.float32)  23.8 us
    dot_general x16, matrix products, opponent_backward(): jnp.dot(opp_second[member].T, incoming[:, member, :], preferred_element_t...  19 us
    all_to_all x4, starting transfers between devices, body(): lax.all_to_all(pack_rows(states[step]), 'pop', split_axis=2, concat_axis=...  18 us
  transfers between devices with their start and end apart: 18, of which 10 were waited for; matrix products, arithmetic and copies ran while one was open for 17% of the time, Pallas kernels for 0%

commit v1 on v0

--- a/solution.py
+++ b/solution.py
@@ -1,9 +1,18 @@
+import functools
 import jax
 import jax.numpy as jnp
 from jax import lax
 from jax.sharding import PartitionSpec as P
 
 CAP = 12
+
+
+def edge_begin(row_data, mesh_ax):
+    mixed_arr = jax.lax.all_gather(row_data, mesh_ax).sum(axis=0)
+    return mixed_arr
+
+
+_compute_goods = functools.partial(edge_begin, mesh_ax="unit")
 
 
 def gru_backward(gradient, pre_gates, latent):
@@ -109,11 +118,10 @@
             scatter_dimension=0,
             tiled=True,
         ).astype(jnp.float32)
-        action_grad = lax.psum(
+        action_grad = _compute_goods(
             jnp.dot(action_flat, flat_grads, preferred_element_type=jnp.float32).astype(
                 jnp.bfloat16
-            ),
-            "unit",
+            )
         ).astype(jnp.float32)
         weight_grad = weight_grad + jnp.dot(
             actions[step], flat_grads.T, preferred_element_type=jnp.float32

time: 742 us -> 669 us (0.902)
  blocking collectives: 290 us -> 102 us
  waiting for transfers between devices: 209 us -> 320 us
    psum x4 -> x0, blocking collectives: 290 us -> none  [body(): lax.psum(jnp.dot(action_flat, flat_grads, preferred_element_type=jnp.floa...]
    all_gather x0 -> x4, blocking collectives: none -> 102 us  [edge_begin(): mixed_arr = jax.lax.all_gather(row_data, mesh_ax).sum(axis=0)]
    reduce_scatter x4, waiting for transfers between devices: 99.7 us -> 157 us  [body(): lax.psum_scatter(jnp.dot(recur_flat, flat_grads, preferred_element_type=j...]
    psum x1, waiting for transfers between devices: 72.7 us -> 123 us  [hidden_slope(): lax.psum(partial_sum.astype(jnp.bfloat16), 'unit').astype(jnp.float32)]
    psum x1, waiting for transfers between devices: 0.01 us -> 8.5 us  [body(): lax.psum(weight_grad.astype(jnp.bfloat16), 'pop').astype(jnp.float32)]
    unnamed x116 -> x120, local copies, waits for them, and re-layouts: 15.6 us -> 16.1 us
  transfers between devices with their start and end apart: 18 -> 18, of which waited for: 10 -> 12; matrix products, arithmetic and copies ran while one was open for 17% -> 19% of each run, Pallas kernels for 0% -> 0%
where the time goes in v1:
time: 669 us; the launch traced here: 661 us
  waiting for transfers between devices  320 us (48%)
  matrix products  114 us (17%)
  blocking collectives  102 us (15%)
  starting transfers between devices  53 us (8%)
  local copies, waits for them, and re-layouts  32 us (5%)
  other arithmetic  24.7 us (4%)
  between operations  15.6 us (2%)
    reduce_scatter x4, waiting for transfers between devices, body(): lax.psum_scatter(jnp.dot(recur_flat, flat_grads, preferred_element_type=j...  157 us
    psum x1, waiting for transfers between devices, hidden_slope(): lax.psum(partial_sum.astype(jnp.bfloat16), 'unit').astype(jnp.float32)  123 us
    all_gather x4, blocking collectives, edge_begin(): mixed_arr = jax.lax.all_gather(row_data, mesh_ax).sum(axis=0)  102 us
    dot_general x16, matrix products, hidden_slope(): jnp.dot(opp_first[member], received[:, member, :], preferred_element_type...  45 us
    dot_general x4, matrix products, body(): jnp.dot(recur_flat, flat_grads, preferred_element_type=jnp.float32)  24 us
    all_to_all x4, waiting for transfers between devices, body(): lax.all_to_all(opponent_backward(slope, incoming, opp_first, opp_second),...  19.3 us
    dot_general x16, matrix products, opponent_backward(): jnp.dot(opp_second[member].T, incoming[:, member, :], preferred_element_t...  19.1 us
    all_to_all x4, starting transfers between devices, body(): lax.all_to_all(pack_rows(states[step]), 'pop', split_axis=2, concat_axis=...  18 us
  transfers between devices with their start and end apart: 18, of which 12 were waited for; matrix products, arithmetic and copies ran while one was open for 19% of the time, Pallas kernels for 0%

profile of v1, /device:TPU:0, one launch (start us, length us, event | category | flops | bytes accessed | tf_op | source)
XLA Modules:
  0.0 661.1 jit_solution(7714859334204871525)
XLA Ops:
  11.7 4.4 all-to-all-start.1
  22.9 4.0 all-to-all-start.4
  34.2 2.4 fusion.39
  37.3 4.8 all-to-all-start.7
  43.7 3.2 fusion.40
  47.0 3.3 fusion.41
  50.2 3.3 fusion.42
  53.5 3.3 fusion.43
  56.7 4.8 all-to-all-start.10
  62.2 3.2 fusion.44
  65.4 3.2 fusion.45
  68.7 3.3 fusion.46
  71.9 3.3 fusion.47
  79.2 2.5 fusion.49
  81.7 2.4 fusion.50
  86.5 3.1 pad_maximum_fusion
  90.0 3.0 pad_maximum_fusion.2
  95.2 28.9 %all-gather = bf16[2048,128]{0,1:T(8,128)(2,1)S(1)} all-gather(bf16[128,128]{0,1:T(8,128)(2,1)S(1)} %fusion.205), channel_id=2, replica_groups=mesh['pop'=8,'unit'=16] {'unit'}, dimensions={0}, use_global_device_ids=true | all-gather | bytes 557056 | tf_op jit(solution)/shard_map/all_gather | solution.py:11
  125.7 5.0 all-to-all-start
  131.3 6.4 fusion.35
  155.4 122.9 %all-reduce.6.cloned.1.call-done = (bf16[4096,384]{0,1:T(8,128)(2,1)}, bf16[4096,384]{0,1:T(8,128)(2,1)}, bf16[4096,384]{0,1:T(8,128)(2,1)}, bf16[4096,384]{0,1:T(8,128)(2,1)}) async-done(((bf16[4096,384]{0,1:T(8,128)(2,1)}, bf16[4096,384]{0,1:T(8,128)(2,1)}, bf16[4096,384]{0,1:T(8,128)(2,1)}, bf16[4096,384]{0,1:T(8,128)(2,1)}), (bf16[4096,384]{0,1:T(8,128)(2,1)}, bf16[4096,384]{0,1:T(8,128)(2,1)}, ...) | async-done | bytes 12582928 | tf_op jit(solution)/shard_map/psum | solution.py:45
  278.3 4.4 fusion.6
  292.1 4.3 all-to-all-start.2
  296.6 6.6 all-to-all-done.2
  303.2 51.3 %reduce-scatter.5.cloned.1.call-done = bf16[256,128]{0,1:T(8,128)(2,1)} async-done(((bf16[4096,128]{0,1:T(8,128)(2,1)}), bf16[256,128]{0,1:T(8,128)(2,1)}) %reduce-scatter.5.cloned.1.call-update) | async-done | bytes 65552 | tf_op jit(solution)/shard_map/reduce_scatter | solution.py:113
  355.9 5.9 fusion.34
  362.0 24.6 %all-gather.1 = bf16[2048,128]{0,1:T(8,128)(2,1)S(1)} all-gather(bf16[128,128]{0,1:T(8,128)(2,1)S(1)} %fusion.204), channel_id=3, replica_groups=mesh['pop'=8,'unit'=16] {'unit'}, dimensions={0}, use_global_device_ids=true | all-gather | bytes 557056 | tf_op jit(solution)/shard_map/all_gather | solution.py:11
  388.1 4.5 all-to-all-start.3
  392.8 5.6 all-to-all-done.3
  402.7 2.7 fusion.13
  408.7 3.4 all-to-all-start.5
  412.4 6.5 all-to-all-done.5
  418.9 15.9 %reduce-scatter.7.cloned.1.call-done = bf16[256,128]{0,1:T(8,128)(2,1)} async-done(((bf16[4096,128]{0,1:T(8,128)(2,1)}), bf16[256,128]{0,1:T(8,128)(2,1)}) %reduce-scatter.7.cloned.1.call-update) | async-done | bytes 65552 | tf_op jit(solution)/shard_map/reduce_scatter | solution.py:113
  436.0 5.9 fusion.33
  442.2 24.6 %all-gather.2 = bf16[2048,128]{0,1:T(8,128)(2,1)S(1)} all-gather(bf16[128,128]{0,1:T(8,128)(2,1)S(1)} %fusion.203), channel_id=4, replica_groups=mesh['pop'=8,'unit'=16] {'unit'}, dimensions={0}, use_global_device_ids=true | all-gather | bytes 557056 | tf_op jit(solution)/shard_map/all_gather | solution.py:11
  468.3 4.2 all-to-all-start.6
  472.7 5.6 all-to-all-done.6
  482.8 2.7 fusion.20
  488.7 3.5 all-to-all-start.8
  492.7 6.3 all-to-all-done.8
  499.0 15.8 %reduce-scatter.9.cloned.1.call-done = bf16[256,128]{0,1:T(8,128)(2,1)} async-done(((bf16[4096,128]{0,1:T(8,128)(2,1)}), bf16[256,128]{0,1:T(8,128)(2,1)}) %reduce-scatter.9.cloned.1.call-update) | async-done | bytes 65552 | tf_op jit(solution)/shard_map/reduce_scatter | solution.py:113
  517.6 24.1 %all-gather.3 = bf16[2048,128]{0,1:T(8,128)(2,1)S(1)} all-gather(bf16[128,128]{0,1:T(8,128)(2,1)S(1)} %fusion.202), channel_id=5, replica_groups=mesh['pop'=8,'unit'=16] {'unit'}, dimensions={0}, use_global_device_ids=true | all-gather | bytes 557056 | tf_op jit(solution)/shard_map/all_gather | solution.py:11
  543.1 4.2 all-to-all-start.9
  547.4 5.9 fusion.32
  557.8 2.7 fusion.27
  563.3 4.8 all-to-all-start.11
  568.1 8.5 %all-reduce.4.cloned.1.call-done = bf16[128,3,256]{2,0,1:T(8,128)(2,1)} async-done(((bf16[128,3,256]{2,0,1:T(8,128)(2,1)}), bf16[128,3,256]{2,0,1:T(8,128)(2,1)}) %all-reduce.4.cloned.1.call-update) | async-done | bytes 196624 | tf_op jit(solution)/shard_map/psum | solution.py:148
  578.3 73.9 %reduce-scatter.11.cloned.1.call-done = bf16[256,128]{0,1:T(8,128)(2,1)} async-done(((bf16[4096,128]{0,1:T(8,128)(2,1)}), bf16[256,128]{0,1:T(8,128)(2,1)}) %reduce-scatter.11.cloned.1.call-update) | async-done | bytes 65552 | tf_op jit(solution)/shard_map/reduce_scatter | solution.py:113
  (256 shorter events, 96.9 us)
Async XLA Ops:
  7.2 87.8 %copy-start = (bf16[128,3,256]{2,0,1:T(8,128)(2,1)S(1)}, bf16[128,3,256]{2,0,1:T(8,128)(2,1)}, u32[]{:S(2)}) copy-start(bf16[128,3,256]{2,0,1:T(8,128)(2,1)} %param.14) | copy-start | bytes 589828
  11.7 11.2 %all-to-all-start.1 = ((bf16[256,4,96]{0,1,2:T(4,128)(2,1)}), bf16[256,4,96]{0,1,2:T(4,128)(2,1)S(1)}, u32[]{:S(2)}, u32[]{:S(2)}) async-start(bf16[256,4,96]{0,1,2:T(4,128)(2,1)} %copy.140), calls=%async_computation.2 | async-start | bytes 393216 | tf_op jit(solution)/shard_map/all_to_all | solution.py:133
  22.9 13.7 %all-to-all-start.4 = ((bf16[256,4,96]{0,1,2:T(4,128)(2,1)}), bf16[256,4,96]{0,1,2:T(4,128)(2,1)S(1)}, u32[]{:S(2)}, u32[]{:S(2)}) async-start(bf16[256,4,96]{0,1,2:T(4,128)(2,1)} %copy.159), calls=%async_computation.6 | async-start | bytes 393216 | tf_op jit(solution)/shard_map/all_to_all | solution.py:133
  37.3 19.5 %all-to-all-start.7 = ((bf16[256,4,96]{0,1,2:T(4,128)(2,1)}), bf16[256,4,96]{0,1,2:T(4,128)(2,1)S(1)}, u32[]{:S(2)}, u32[]{:S(2)}) async-start(bf16[256,4,96]{0,1,2:T(4,128)(2,1)} %copy.178), calls=%async_computation.10 | async-start | bytes 393216 | tf_op jit(solution)/shard_map/all_to_all | solution.py:133
  56.7 18.5 %all-to-all-start.10 = ((bf16[256,4,96]{0,1,2:T(4,128)(2,1)}), bf16[256,4,96]{0,1,2:T(4,128)(2,1)}, u32[]{:S(2)}, u32[]{:S(2)}) async-start(bf16[256,4,96]{0,1,2:T(4,128)(2,1)} %copy.197), calls=%async_computation.14 | async-start | bytes 393216 | tf_op jit(solution)/shard_map/all_to_all | solution.py:133
  61.6 216.8 %all-reduce.6.cloned.1.call-start = ((), (), s32[]{:S(2)}) async-start(), calls=%async_computation.21 | async-start | bytes 25165824 | tf_op jit(solution)/shard_map/psum | solution.py:45
  79.2 7.3 %copy-start.5 = (bf16[4096,96]{0,1:T(8,128)(2,1)S(1)}, bf16[4096,96]{0,1:T(8,128)(2,1)}, u32[]{:S(2)}) copy-start(bf16[4096,96]{0,1:T(8,128)(2,1)} %fusion.40) | copy-start | bytes 2359300
  79.2 7.3 %copy-start.6 = (bf16[4096,96]{0,1:T(8,128)(2,1)S(1)}, bf16[4096,96]{0,1:T(8,128)(2,1)}, u32[]{:S(2)}) copy-start(bf16[4096,96]{0,1:T(8,128)(2,1)} %fusion.41) | copy-start | bytes 2359300
  79.2 7.3 %copy-start.7 = (bf16[4096,96]{0,1:T(8,128)(2,1)S(1)}, bf16[4096,96]{0,1:T(8,128)(2,1)}, u32[]{:S(2)}) copy-start(bf16[4096,96]{0,1:T(8,128)(2,1)} %fusion.42) | copy-start | bytes 2359300
  79.2 7.3 %copy-start.8 = (bf16[4096,96]{0,1:T(8,128)(2,1)S(1)}, bf16[4096,96]{0,1:T(8,128)(2,1)}, u32[]{:S(2)}) copy-start(bf16[4096,96]{0,1:T(8,128)(2,1)} %fusion.43) | copy-start | bytes 2359300
  94.1 30.1 %copy-start.19 = (bf16[4,128,128]{2,1,0:T(8,128)(2,1)S(1)}, bf16[4,128,128]{2,1,0:T(8,128)(2,1)}, u32[]{:S(2)}) copy-start(bf16[4,128,128]{2,1,0:T(8,128)(2,1)} %param.11) | copy-start | bytes 393220
  94.3 29.8 %copy-start.33 = (bf16[1,1,256,128]{2,3,1,0:T(8,128)(2,1)}, bf16[1,1,256,128]{2,3,1,0:T(8,128)(2,1)S(1)}, u32[]{:S(2)}) copy-start(bf16[1,1,256,128]{2,3,1,0:T(8,128)(2,1)S(1)} %copy.215) | copy-start | bytes 196612
  94.8 29.3 %copy-start.35 = (bf16[256,128]{0,1:T(8,128)(2,1)}, bf16[256,128]{0,1:T(8,128)(2,1)S(1)}, u32[]{:S(2)}) copy-start(bf16[256,128]{0,1:T(8,128)(2,1)S(1)} %copy.128) | copy-start | bytes 196612
  125.7 23.1 %all-to-all-start = ((bf16[128,4,96]{0,1,2:T(4,128)(2,1)}), bf16[128,4,96]{0,1,2:T(4,128)(2,1)S(1)}, u32[]{:S(2)}, u32[]{:S(2)}) async-start(bf16[128,4,96]{0,1,2:T(4,128)(2,1)} %copy.135), calls=%async_computation.1 | async-start | bytes 196608 | tf_op jit(solution)/shard_map/all_to_all | solution.py:134
  130.7 223.9 %reduce-scatter.5.cloned.1.call-start = ((), (), s32[]{:S(2)}) async-start(), calls=%async_computation.16 | async-start | bytes 1114112 | tf_op jit(solution)/shard_map/reduce_scatter | solution.py:113
  148.8 3.6 copy-start.1
  286.9 9.5 %copy-start.20 = (bf16[4,128,128]{2,1,0:T(8,128)(2,1)S(1)}, bf16[4,128,128]{2,1,0:T(8,128)(2,1)}, u32[]{:S(2)}) copy-start(bf16[4,128,128]{2,1,0:T(8,128)(2,1)} %param.11) | copy-start | bytes 393220
  286.9 67.7 %copy-start.34 = (bf16[1,1,256,128]{2,3,1,0:T(8,128)(2,1)S(1)}, bf16[1,1,256,128]{2,3,1,0:T(8,128)(2,1)}, u32[]{:S(2)}) copy-start(bf16[1,1,256,128]{2,3,1,0:T(8,128)(2,1)} %copy-done.33) | copy-start | bytes 196612
  286.9 67.7 %copy-start.36 = (bf16[256,128]{0,1:T(8,128)(2,1)S(1)}, bf16[256,128]{0,1:T(8,128)(2,1)}, u32[]{:S(2)}) copy-start(bf16[256,128]{0,1:T(8,128)(2,1)} %copy-done.35) | copy-start | bytes 196612
  289.1 66.6 %copy-start.26 = (bf16[1,1,256,128]{2,3,1,0:T(8,128)(2,1)S(1)}, bf16[1,1,256,128]{2,3,1,0:T(8,128)(2,1)}, u32[]{:S(2)}) copy-start(bf16[1,1,256,128]{2,3,1,0:T(8,128)(2,1)} %copy.228) | copy-start | bytes 196612
  289.1 66.6 %copy-start.30 = (bf16[1,1,256,128]{2,3,1,0:T(8,128)(2,1)S(1)}, bf16[1,1,256,128]{2,3,1,0:T(8,128)(2,1)}, u32[]{:S(2)}) copy-start(bf16[1,1,256,128]{2,3,1,0:T(8,128)(2,1)} %copy.229) | copy-start | bytes 196612
  289.1 66.6 %copy-start.31 = (bf16[1,1,256,128]{2,3,1,0:T(8,128)(2,1)S(1)}, bf16[1,1,256,128]{2,3,1,0:T(8,128)(2,1)}, u32[]{:S(2)}) copy-start(bf16[1,1,256,128]{2,3,1,0:T(8,128)(2,1)} %copy.230) | copy-start | bytes 196612
  289.1 66.6 %copy-start.32 = (bf16[1,256,128]{1,2,0:T(8,128)(2,1)S(1)}, bf16[1,256,128]{1,2,0:T(8,128)(2,1)}, u32[]{:S(2)}) copy-start(bf16[1,256,128]{1,2,0:T(8,128)(2,1)} %copy.231) | copy-start | bytes 196612
  292.1 11.1 %all-to-all-start.2 = ((bf16[256,4,96]{0,1,2:T(4,128)(2,1)}), bf16[256,4,96]{0,1,2:T(4,128)(2,1)S(1)}, u32[]{:S(2)}, u32[]{:S(2)}) async-start(bf16[256,4,96]{0,1,2:T(4,128)(2,1)} %copy.145), calls=%async_computation.3 | async-start | bytes 393216 | tf_op jit(solution)/shard_map/all_to_all | solution.py:137
  296.4 138.4 %reduce-scatter.7.cloned.1.call-start = ((), (), s32[]{:S(2)}) async-start(), calls=%async_computation.17 | async-start | bytes 1114112 | tf_op jit(solution)/shard_map/reduce_scatter | solution.py:113
  355.9 31.1 %copy-start.39 = (bf16[1,128,128]{1,2,0:T(8,128)(2,1)S(1)}, bf16[1,128,128]{1,2,0:T(8,128)(2,1)}, u32[]{:S(2)}) copy-start(bf16[1,128,128]{1,2,0:T(8,128)(2,1)} %copy.232) | copy-start | bytes 98308
  388.1 10.2 %all-to-all-start.3 = ((bf16[128,4,96]{0,1,2:T(4,128)(2,1)}), bf16[128,4,96]{0,1,2:T(4,128)(2,1)S(1)}, u32[]{:S(2)}, u32[]{:S(2)}) async-start(bf16[128,4,96]{0,1,2:T(4,128)(2,1)} %copy.154), calls=%async_computation.5 | async-start | bytes 196608 | tf_op jit(solution)/shard_map/all_to_all | solution.py:134
  398.3 3.6 copy-start.2
  407.3 28.5 %copy-start.22 = (bf16[1,1,256,128]{2,3,1,0:T(8,128)(2,1)S(1)}, bf16[1,1,256,128]{2,3,1,0:T(8,128)(2,1)}, u32[]{:S(2)}) copy-start(bf16[1,1,256,128]{2,3,1,0:T(8,128)(2,1)} %copy.241) | copy-start | bytes 196612
  407.3 28.5 %copy-start.27 = (bf16[1,1,256,128]{2,3,1,0:T(8,128)(2,1)S(1)}, bf16[1,1,256,128]{2,3,1,0:T(8,128)(2,1)}, u32[]{:S(2)}) copy-start(bf16[1,1,256,128]{2,3,1,0:T(8,128)(2,1)} %copy.242) | copy-start | bytes 196612
  407.3 28.5 %copy-start.28 = (bf16[1,1,256,128]{2,3,1,0:T(8,128)(2,1)S(1)}, bf16[1,1,256,128]{2,3,1,0:T(8,128)(2,1)}, u32[]{:S(2)}) copy-start(bf16[1,1,256,128]{2,3,1,0:T(8,128)(2,1)} %copy.243) | copy-start | bytes 196612
  407.3 28.5 %copy-start.29 = (bf16[1,256,128]{1,2,0:T(8,128)(2,1)S(1)}, bf16[1,256,128]{1,2,0:T(8,128)(2,1)}, u32[]{:S(2)}) copy-start(bf16[1,256,128]{1,2,0:T(8,128)(2,1)} %copy.244) | copy-start | bytes 196612
  408.7 10.2 %all-to-all-start.5 = ((bf16[256,4,96]{0,1,2:T(4,128)(2,1)}), bf16[256,4,96]{0,1,2:T(4,128)(2,1)S(1)}, u32[]{:S(2)}, u32[]{:S(2)}) async-start(bf16[256,4,96]{0,1,2:T(4,128)(2,1)} %copy.164), calls=%async_computation.7 | async-start | bytes 393216 | tf_op jit(solution)/shard_map/all_to_all | solution.py:137
  412.1 102.7 %reduce-scatter.9.cloned.1.call-start = ((), (), s32[]{:S(2)}) async-start(), calls=%async_computation.18 | async-start | bytes 1114112 | tf_op jit(solution)/shard_map/reduce_scatter | solution.py:113
  436.0 31.2 %copy-start.38 = (bf16[1,128,128]{1,2,0:T(8,128)(2,1)S(1)}, bf16[1,128,128]{1,2,0:T(8,128)(2,1)}, u32[]{:S(2)}) copy-start(bf16[1,128,128]{1,2,0:T(8,128)(2,1)} %copy.245) | copy-start | bytes 98308
  468.3 10.0 %all-to-all-start.6 = ((bf16[128,4,96]{0,1,2:T(4,128)(2,1)}), bf16[128,4,96]{0,1,2:T(4,128)(2,1)S(1)}, u32[]{:S(2)}, u32[]{:S(2)}) async-start(bf16[128,4,96]{0,1,2:T(4,128)(2,1)} %copy.173), calls=%async_computation.9 | async-start | bytes 196608 | tf_op jit(solution)/shard_map/all_to_all | solution.py:134
  478.3 3.6 copy-start.3
  487.3 28.6 %copy-start.21 = (bf16[1,1,256,128]{2,3,1,0:T(8,128)(2,1)S(1)}, bf16[1,1,256,128]{2,3,1,0:T(8,128)(2,1)}, u32[]{:S(2)}) copy-start(bf16[1,1,256,128]{2,3,1,0:T(8,128)(2,1)} %copy.254) | copy-start | bytes 196612
  487.3 28.6 %copy-start.23 = (bf16[1,1,256,128]{2,3,1,0:T(8,128)(2,1)S(1)}, bf16[1,1,256,128]{2,3,1,0:T(8,128)(2,1)}, u32[]{:S(2)}) copy-start(bf16[1,1,256,128]{2,3,1,0:T(8,128)(2,1)} %copy.255) | copy-start | bytes 196612
  487.3 28.6 %copy-start.24 = (bf16[1,1,256,128]{2,3,1,0:T(8,128)(2,1)S(1)}, bf16[1,1,256,128]{2,3,1,0:T(8,128)(2,1)}, u32[]{:S(2)}) copy-start(bf16[1,1,256,128]{2,3,1,0:T(8,128)(2,1)} %copy.256) | copy-start | bytes 196612
  487.4 28.6 %copy-start.25 = (bf16[1,256,128]{1,2,0:T(8,128)(2,1)S(1)}, bf16[1,256,128]{1,2,0:T(8,128)(2,1)}, u32[]{:S(2)}) copy-start(bf16[1,256,128]{1,2,0:T(8,128)(2,1)} %copy.257) | copy-start | bytes 196612
  488.7 53.3 %copy-start.37 = (bf16[1,128,128]{1,2,0:T(8,128)(2,1)S(1)}, bf16[1,128,128]{1,2,0:T(8,128)(2,1)}, u32[]{:S(2)}) copy-start(bf16[1,128,128]{1,2,0:T(8,128)(2,1)} %copy.258) | copy-start | bytes 98308
  488.7 10.3 %all-to-all-start.8 = ((bf16[256,4,96]{0,1,2:T(4,128)(2,1)}), bf16[256,4,96]{0,1,2:T(4,128)(2,1)S(1)}, u32[]{:S(2)}, u32[]{:S(2)}) async-start(bf16[256,4,96]{0,1,2:T(4,128)(2,1)} %copy.183), calls=%async_computation.11 | async-start | bytes 393216 | tf_op jit(solution)/shard_map/all_to_all | solution.py:137
  492.2 84.3 %all-reduce.4.cloned.1.call-start = ((), (), s32[]{:S(2)}) async-start(), calls=%async_computation.20 | async-start | bytes 393216 | tf_op jit(solution)/shard_map/psum | solution.py:148
  543.1 10.2 %all-to-all-start.9 = ((bf16[128,4,96]{0,1,2:T(4,128)(2,1)}), bf16[128,4,96]{0,1,2:T(4,128)(2,1)S(1)}, u32[]{:S(2)}, u32[]{:S(2)}) async-start(bf16[128,4,96]{0,1,2:T(4,128)(2,1)} %copy.192), calls=%async_computation.13 | async-start | bytes 196608 | tf_op jit(solution)/shard_map/all_to_all | solution.py:134
  547.4 104.9 %reduce-scatter.11.cloned.1.call-start = ((), (), s32[]{:S(2)}) async-start(), calls=%async_computation.19 | async-start | bytes 1114112 | tf_op jit(solution)/shard_map/reduce_scatter | solution.py:113
  553.3 3.7 copy-start.4
  563.3 15.0 %all-to-all-start.11 = ((bf16[256,4,96]{0,1,2:T(4,128)(2,1)}), bf16[256,4,96]{0,1,2:T(4,128)(2,1)S(1)}, u32[]{:S(2)}, u32[]{:S(2)}) async-start(bf16[256,4,96]{0,1,2:T(4,128)(2,1)} %copy.202), calls=%async_computation.15 | async-start | bytes 393216 | tf_op jit(solution)/shard_map/all_to_all | solution.py:137
  (17 other events, 44.2 us)
Sparse Core Ops, SparseCore 0:
  93.1 185.1 all-reduce.5
  281.8 72.6 reduce-scatter.4
  362.1 72.5 reduce-scatter.6
  442.3 72.4 reduce-scatter.8
  517.7 58.8 all-reduce.3
  580.0 72.2 reduce-scatter.10
